TPU v7x, 256 devices: a whole 4x4x8 slice. The times are simulated.
256 devices in a mesh: dp: 4 (over y), tensor: 64 (over x, z, core).
Axes of the slice: x: 4, y: 4, z: 8, core: 2. Of those that a mesh axis runs over, the one named last changes fastest.
Arguments:
- tokens: bfloat16 [4, 8192, 1536], P('dp', 'tensor'), may hold values from -6 to 6
- attn_gain: float32 [1536], replicated, may hold values from 0.1 to 1.9
- qkv_weight: bfloat16 [1536, 2560], P(None, 'dp'), may hold values from -0.25 to 0.25
- out_weight: bfloat16 [1536, 1536], P('dp'), may hold values from -0.15625 to 0.15625
- prefix_cache: bfloat16 [4, 512, 2, 512], P('dp', 'tensor'), may hold values from -640 to 640
- lengths: int32 [4, 256], P('dp'), may hold values from 1 to 384, 8192 in all within a row
- ffn_gain: float32 [1536], replicated, may hold values from 0.1 to 1.9
- expert_ids: int32 [4, 8192, 8], P('dp', 'tensor'), may hold values from 0 to 31, all different within a row; in each aligned block of 128 rows (0 to 127, 128 to 255, ..., all dimensions but the last counted through in order) at most 40 rows name the same one
- gate_weights: float32 [4, 8192, 8], P('dp', 'tensor'), may hold values from 0.05 to 0.5
- expert_in: bfloat16 [64, 1536, 512], P('tensor'), may hold values from -0.15625 to 0.15625
- expert_out: bfloat16 [64, 256, 1536], P('tensor'), may hold values from -0.25 to 0.25
Outputs:
- hidden_state: bfloat16 [4, 8192, 1536], P('dp', 'tensor')
- mixed: bfloat16 [4, 8192, 1536], P('dp', 'tensor')
Inputs may be any that keep to these rules, and one draw needn't show every extreme that they name: `lengths`: each group's 256 requests fill its 8192 suffix positions in order, and the longest holds exactly 384 tokens. `expert_ids`: each token names 8 different experts; among the 128 tokens of one device no expert is named more than 40 times, a bound that some block reaches.
All inputs are finite; a program needn't handle non-finite values.
Results may differ from a plain program's by a relative error of at most 0.014.
The roundings to bfloat16 on the way count: a program that leaves them out, or rounds other values in their place, can miss the bound.
Values may be sent and summed in bfloat16 or wider, within the bound.
No kernel may reach another device: no remote copies, remote signals or barrier semaphores. Data moves between devices by JAX's collectives and lax.ppermute only.
A program may use at most 128 MiB of HBM per device.

v0:
```python
import jax
import jax.numpy as jnp
from jax import lax
from jax.sharding import PartitionSpec as P

HEADS = 24
KV_HEADS = 8
HEAD_DIM = 64
EXPERTS = 32
TOPK = 8
SHIFTS = 2
CAP = 40
EPS = 1e-06
THETA = 10000.0


def from_behind(value, axis, steps):
    count = lax.axis_size(axis)
    first, last = (max(0, -steps), min(count, count - steps))
    return lax.ppermute(value, axis, [(source, source + steps) for source in range(first, last)])


def rms_norm(x, gain):
    values = x.astype(jnp.float32)
    mean_sq = jnp.mean(values * values, axis=-1, keepdims=True)
    return (values * lax.rsqrt(mean_sq + EPS) * gain).astype(jnp.bfloat16)


def rotary(x, positions):
    half = x.shape[-1] // 2
    freqs = THETA ** (-jnp.arange(half, dtype=jnp.float32) * 2.0 / x.shape[-1])
    angles = positions.astype(jnp.float32)[:, None] * freqs[None, :]
    cosine = jnp.concatenate([jnp.cos(angles), jnp.cos(angles)], axis=-1)[:, None, :]
    sine = jnp.concatenate([jnp.sin(angles), jnp.sin(angles)], axis=-1)[:, None, :]
    turned = jnp.concatenate([-x[..., half:], x[..., :half]], axis=-1)
    return x * cosine + turned * sine


def request_info(index, lengths):
    ends = jnp.cumsum(lengths, dtype=jnp.int32)
    before = ends[None, :] <= index[:, None]
    segment = jnp.sum(before.astype(jnp.int32), axis=1, dtype=jnp.int32)
    start = jnp.sum(jnp.where(before, lengths[None, :], 0), axis=1, dtype=jnp.int32)
    return (segment, index - start)


def merge_block(carry, scores, values, visible):
    best, total, acc = carry
    if visible is not None:
        scores = jnp.where(visible, scores, -1e30)
    newest = jnp.maximum(best, jnp.max(scores, axis=-1))
    probs = jnp.exp(scores - newest[..., None])
    if visible is not None:
        probs = jnp.where(visible, probs, 0.0)
    decay = jnp.exp(best - newest)
    total = total * decay + jnp.sum(probs, axis=-1)
    acc = acc * decay[..., None] + jnp.einsum(
        "tgrn,ngd->tgrd", probs.astype(jnp.bfloat16), values, preferred_element_type=jnp.float32
    )
    return (newest, total, acc)


def shards(
    tokens,
    attn_gain,
    qkv_weight,
    out_weight,
    prefix_cache,
    lengths,
    ffn_gain,
    expert_ids,
    gate_weights,
    expert_in,
    expert_out,
):
    rows = tokens.shape[1]
    model = tokens.shape[2]
    head_cols = HEADS * HEAD_DIM
    kv_cols = KV_HEADS * HEAD_DIM
    ratio = HEADS // KV_HEADS
    scale = 1.0 / HEAD_DIM**0.5
    lanes = lax.axis_size("tensor")
    prefix_len = prefix_cache.shape[1] * lanes
    own_lengths = lengths[0]
    inputs = tokens[0]
    normed = rms_norm(inputs, attn_gain)
    full_qkv, full_out = (
        lax.all_gather(qkv_weight, "dp", axis=1, tiled=True),
        lax.all_gather(out_weight, "dp", axis=0, tiled=True),
    )
    qkv = jnp.dot(normed, full_qkv, preferred_element_type=jnp.float32).astype(jnp.bfloat16)
    lane = lax.axis_index("tensor")
    q_index = lane * rows + jnp.arange(rows, dtype=jnp.int32)
    q_segment, offset = request_info(q_index, own_lengths)
    positions = prefix_len + offset
    query = rotary(
        qkv[:, :head_cols].astype(jnp.float32).reshape(rows, HEADS, HEAD_DIM), positions
    ).astype(jnp.bfloat16)
    query = query.reshape(rows, KV_HEADS, ratio, HEAD_DIM)
    keys = rotary(
        qkv[:, head_cols : head_cols + kv_cols]
        .astype(jnp.float32)
        .reshape(rows, KV_HEADS, HEAD_DIM),
        positions,
    ).astype(jnp.bfloat16)
    local_pairs = jnp.stack([keys.reshape(rows, kv_cols), qkv[:, head_cols + kv_cols :]], axis=1)
    start_carry = (
        jnp.full((rows, KV_HEADS, ratio), -1e30, jnp.float32),
        jnp.zeros((rows, KV_HEADS, ratio), jnp.float32),
        jnp.zeros((rows, KV_HEADS, ratio, HEAD_DIM), jnp.float32),
    )
    piece = lax.all_gather(prefix_cache[0], "tensor", axis=0, tiled=True)
    count = piece.shape[0]
    cached_keys = piece[:, 0].reshape(count, KV_HEADS, HEAD_DIM)
    cached_values = piece[:, 1].reshape(count, KV_HEADS, HEAD_DIM)
    scores = (
        jnp.einsum("tgrd,ngd->tgrn", query, cached_keys, preferred_element_type=jnp.float32) * scale
    )
    carry = merge_block(start_carry, scores, cached_values, None)
    window = local_pairs[None]
    for bit in range(SHIFTS):
        earlier = from_behind(window, "tensor", 2**bit)
        window = jnp.concatenate([window, earlier], axis=0)
    depth = window.shape[0]
    k_index = (
        (lane - jnp.arange(depth, dtype=jnp.int32))[:, None] * rows
        + jnp.arange(rows, dtype=jnp.int32)[None, :]
    ).reshape(-1)
    k_segment, unused = request_info(k_index, own_lengths)
    visible = (
        (k_index[None, :] >= 0)
        & (k_index[None, :] <= q_index[:, None])
        & (k_segment[None, :] == q_segment[:, None])
    )
    suffix_pairs = window.reshape(depth * rows, 2, kv_cols)
    suffix_keys = suffix_pairs[:, 0].reshape(depth * rows, KV_HEADS, HEAD_DIM)
    suffix_values = suffix_pairs[:, 1].reshape(depth * rows, KV_HEADS, HEAD_DIM)
    scores = (
        jnp.einsum("tgrd,ngd->tgrn", query, suffix_keys, preferred_element_type=jnp.float32) * scale
    )
    best, total, acc = merge_block(carry, scores, suffix_values, visible[:, None, None, :])
    attended = (acc / total[..., None]).astype(jnp.bfloat16).reshape(rows, head_cols)
    projected = jnp.dot(attended, full_out, preferred_element_type=jnp.float32)
    hidden_state = (inputs.astype(jnp.float32) + projected).astype(jnp.bfloat16)
    moe_input = rms_norm(hidden_state, ffn_gain)
    total_units = expert_in.shape[0] * lanes
    parts = total_units // EXPERTS
    unit_ff = expert_in.shape[2] // 2
    flat_ids = expert_ids[0].reshape(-1)
    onehot = (flat_ids[:, None] == jnp.arange(EXPERTS, dtype=jnp.int32)[None, :]).astype(jnp.int32)
    earlier_count = jnp.cumsum(onehot, axis=0, dtype=jnp.int32) - onehot
    slots = jnp.sum(earlier_count * onehot, axis=1, dtype=jnp.int32)
    unit_ids = flat_ids[:, None] * parts + jnp.arange(parts, dtype=jnp.int32)[None, :]
    target = (unit_ids * CAP + slots[:, None]).reshape(-1)
    row_of = jnp.repeat(jnp.arange(rows, dtype=jnp.int32), TOPK * parts)
    source = jnp.full((total_units * CAP,), rows, jnp.int32).at[target].set(row_of)
    padded_input = jnp.concatenate([moe_input, jnp.zeros((1, model), jnp.bfloat16)], axis=0)
    outgoing = padded_input[source]
    arrived = lax.all_to_all(
        outgoing.reshape(total_units, CAP, model), "tensor", split_axis=0, concat_axis=1, tiled=True
    )
    inner = jnp.einsum("erd,edf->erf", arrived, expert_in, preferred_element_type=jnp.float32)
    activated = (jax.nn.silu(inner[..., :unit_ff]) * inner[..., unit_ff:]).astype(jnp.bfloat16)
    produced = jnp.einsum(
        "erf,efd->erd", activated, expert_out, preferred_element_type=jnp.float32
    ).astype(jnp.bfloat16)
    returned = lax.all_to_all(produced, "tensor", split_axis=1, concat_axis=0, tiled=True)
    picked = returned.reshape(total_units * CAP, model)[target].reshape(rows, TOPK, parts, model)
    combined = jnp.einsum("tk,tksd->td", gate_weights[0], picked.astype(jnp.float32))
    mixed = (hidden_state.astype(jnp.float32) + combined).astype(jnp.bfloat16)
    return (hidden_state[None], mixed[None])


def solution(mesh):
    in_specs = (
        P("dp", "tensor", None),
        P(),
        P(None, "dp"),
        P("dp", None),
        P("dp", "tensor", None, None),
        P("dp", None),
        P(),
        P("dp", "tensor", None),
        P("dp", "tensor", None),
        P("tensor", None, None),
        P("tensor", None, None),
    )
    out_specs = (P("dp", "tensor", None), P("dp", "tensor", None))
    return jax.shard_map(shards, mesh=mesh, in_specs=in_specs, out_specs=out_specs, check_vma=False)
```

profile of v0, /device:TPU:1, one launch (start us, length us, event | category | flops | bytes accessed | tf_op | source)
XLA Modules:
  0.0 881.9 jit_solution(11526907995774648510)
XLA Ops:
  14.2 9.0 %reduce-window.19 = s32[32,8,128]{2,1,0:T(8,128)S(1)} reduce-window(s32[32,8,128]{2,1,0:T(8,128)S(1)} %fusion.61, s32[]{:T(128)} %constant.24.clone.1), window={size=1x1x128 pad=0_0x0_0x127_0}, to_apply=%region_11.12 | reduce-window | flops 4161536 | bytes 262148 | tf_op jit(solution)/shard_map/reduce-window.2
  24.5 8.1 scatter_custom_fusion
  34.4 57.4 %all-gather.9.cloned.1.call-done = bf16[1,512,2,512]{3,2,0,1:T(2,128)(2,1)} async-done(((bf16[1,8,2,512]{3,2,0,1:T(2,128)(2,1)}), bf16[1,512,2,512]{3,2,0,1:T(2,128)(2,1)}) %all-gather.9.cloned.1.call-update) | async-done | bytes 1048592 | tf_op jit(solution)/shard_map/all_gather | solution.py:112
  91.8 4.2 fusion.70
  96.0 3.5 copy.73
  99.5 3.5 copy.74
  103.0 69.1 %all-gather.5.cloned.1.call-done = bf16[1536,2560]{1,0:T(8,128)(2,1)} async-done(((bf16[1536,640]{1,0:T(8,128)(2,1)}), bf16[1536,2560]{1,0:T(8,128)(2,1)}) %all-gather.5.cloned.1.call-update) | async-done | bytes 7864336 | tf_op jit(solution)/shard_map/all_gather | solution.py:88
  172.1 4.5 convolution_convert_fusion.1
  178.5 3.9 collective-permute-start
  182.9 3.2 collective-permute-done
  187.2 3.7 collective-permute-start.1
  191.8 4.8 bitcast_reduce_fusion
  196.6 3.7 collective-permute-done.1
  203.8 2.1 copy.80
  207.0 3.7 fusion.3
  217.0 13.0 %all-gather.7.cloned.1.call-done = bf16[1536,1536]{1,0:T(8,128)(2,1)} async-done(((bf16[384,1536]{1,0:T(8,128)(2,1)}), bf16[1536,1536]{1,0:T(8,128)(2,1)}) %all-gather.7.cloned.1.call-update) | async-done | bytes 4718608 | tf_op jit(solution)/shard_map/all_gather | solution.py:89
  230.0 3.2 fusion.40
  233.5 9.5 %gather_fusion = bf16[2560,1536]{1,0:T(8,128)(2,1)} fusion(bf16[129,1536]{1,0:T(8,128)(2,1)S(1)} %concatenate.37, s32[3072]{0:T(1024)S(1)} %pad_clamp_fusion), kind=kCustom, calls=%fused_computation | custom fusion | bytes 15738880 | tf_op jit(solution)/shard_map/gather | solution.py:158
  243.0 185.6 %all_to_all.8 = bf16[64,40,1536]{2,1,0:T(8,128)(2,1)S(1)} all-to-all(bf16[64,40,1536]{2,1,0:T(8,128)(2,1)} %bitcast.167), channel_id=1, replica_groups=mesh['dp'=4,'tensor'=64] {'tensor'}, dimensions={0} | all-to-all | bytes 15728640 | tf_op jit(solution)/shard_map/all_to_all | solution.py:159
  428.6 4.2 convolution_bitcast_fusion
  432.8 2.3 fusion
  435.1 86.3 %copy.103 = bf16[1,2560,1536]{2,0,1:T(2,128)(2,1)} copy(bf16[1,2560,1536]{2,1,0:T(8,128)(2,1)S(1)} %fusion) | data formatting | bytes 15728640 | tf_op jit(solution)/shard_map/convert_element_type | solution.py:166
  522.0 51.5 %reduce.2 = bf16[2560,1536]{1,0:T(8,128)(2,1)} reduce(bf16[2560,1,1536]{2,1,0:T(2,128)(2,1)} %bitcast.165, bf16[]{:T(256)} %broadcast.284), dimensions={1}, to_apply=%bitcast.163.reduce_sub_computation | reduce | bytes 15728642
  573.5 17.7 %reshape.394 = bf16[64,2,30720]{2,1,0:T(2,128)(2,1)} reshape(bf16[2560,1536]{1,0:T(8,128)(2,1)} %reduce.2) | data formatting | bytes 15728640
  591.1 6.4 all-to-all-start.1
  597.8 174.3 %all-to-all-done.1 = bf16[64,2,30720]{2,1,0:T(2,128)(2,1)} async-done(((bf16[64,2,30720]{2,1,0:T(2,128)(2,1)}), bf16[64,2,30720]{2,1,0:T(2,128)(2,1)}, u32[]{:S(2)}, u32[]{:S(2)}) %all-to-all-start.1) | async-done | bytes 7864352 | tf_op jit(solution)/shard_map/all_to_all | solution.py:167
  772.1 38.0 %reshape.395 = bf16[2560,1,1536]{2,1,0:T(2,128)(2,1)} reshape(bf16[64,2,30720]{2,1,0:T(2,128)(2,1)} %all-to-all-done.1) | data formatting | bytes 15728640
  810.1 10.8 %copy.102 = bf16[1,2560,1536]{2,1,0:T(8,128)(2,1)} copy(bf16[1,2560,1536]{2,0,1:T(2,128)(2,1)} %bitcast.166) | data formatting | bytes 15728640
  820.9 17.5 %gather_fusion.1 = bf16[2048,1536]{1,0:T(8,128)(2,1)} fusion(bf16[2560,1536]{1,0:T(8,128)(2,1)} %bitcast.164, s32[2048]{0:T(1024)S(1)} %broadcast_clamp_fusion), kind=kCustom, calls=%fused_computation.1 | custom fusion | bytes 12591104 | tf_op jit(solution)/shard_map/gather | solution.py:168
  838.4 14.1 %reshape.358 = f32[128,8,2,1536]{3,2,1,0:T(2,128)} reshape(bf16[2048,1536]{1,0:T(8,128)(2,1)} %gather_fusion.1) | data formatting | bytes 18874368 | tf_op jit(solution)/shard_map/convert_element_type | solution.py:169
  852.6 18.9 %reduce_sum.89 = bf16[128,8,1536]{2,1,0:T(8,128)(2,1)} reduce(f32[128,8,2,1536]{3,2,1,0:T(2,128)} %reshape.358, f32[]{:T(128)} %constant.19.clone.1), dimensions={2}, to_apply=%region_15.16 | reduce | flops 1572864 | bytes 15728644 | tf_op jit(solution)/shard_map/tk,tksd->td/reduce_sum | solution.py:169
  871.4 2.8 fusion.72
  (107 shorter events, 26.7 us)
Async XLA Ops:
  7.2 421.4 %copy-start = (bf16[1,1536,512]{2,1,0:T(8,128)(2,1)S(1)}, bf16[1,1536,512]{2,1,0:T(8,128)(2,1)}, u32[]{:S(2)}) copy-start(bf16[1,1536,512]{2,1,0:T(8,128)(2,1)} %param.20) | copy-start | bytes 4718596
  7.2 84.6 %all-gather.9.cloned.1.call-start = ((), (), s32[]{:S(2)}) async-start(), calls=%async_computation.4 | async-start | bytes 1064960 | tf_op jit(solution)/shard_map/all_gather | solution.py:112
  7.9 164.2 %all-gather.5.cloned.1.call-start = ((), (), s32[]{:S(2)}) async-start(), calls=%async_computation.2 | async-start | bytes 9830400 | tf_op jit(solution)/shard_map/all_gather | solution.py:88
  8.7 163.5 %copy-start.2 = (bf16[1,128,1536]{2,1,0:T(8,128)(2,1)S(1)}, bf16[1,128,1536]{2,1,0:T(8,128)(2,1)}, u32[]{:S(2)}) copy-start(bf16[1,128,1536]{2,1,0:T(8,128)(2,1)} %param.11) | copy-start | bytes 1179652
  8.7 163.4 %copy-start.8 = (f32[1536]{0:T(1024)S(1)}, f32[1536]{0:T(1024)}, u32[]{:S(2)}) copy-start(f32[1536]{0:T(1024)} %param.12) | copy-start | bytes 18436
  8.7 221.3 %all-gather.7.cloned.1.call-start = ((), (), s32[]{:S(2)}) async-start(), calls=%async_computation.3 | async-start | bytes 5898240 | tf_op jit(solution)/shard_map/all_gather | solution.py:89
  24.4 8.2 copy-start.9
  34.2 68.8 %copy-start.7 = (f32[128,64]{0,1:T(8,128)}, f32[128,64]{0,1:T(8,128)S(1)}, u32[]{:S(2)}) copy-start(f32[128,64]{0,1:T(8,128)S(1)} %get-tuple-element.27) | copy-start | bytes 98308
  178.5 7.5 collective-permute-start
  187.2 13.1 %collective-permute-start.1 = (bf16[2,128,2,512]{3,1,2,0:T(8,128)(2,1)S(1)}, bf16[2,128,2,512]{3,1,2,0:T(8,128)(2,1)S(1)}, u32[]{:S(2)}, u32[]{:S(2)}) collective-permute-start(bf16[2,128,2,512]{3,1,2,0:T(8,128)(2,1)S(1)} %pad_maximum_fusion.1), channel_id=1, source_target_pairs={{0,2},{1,3},{2,4},{3,5},{4,6},{5,7},{6,8},{7,9},{8,10},{9,11},{10,... | collective-permute-start | bytes 1572872 | tf_op jit(solution)/shard_map/ppermute | solution.py:20
  191.8 14.1 %copy-start.4 = (pred[128,512]{0,1:T(8,128)(4,1)S(1)}, pred[128,512]{0,1:T(8,128)(4,1)}, u32[]{:S(2)}) copy-start(pred[128,512]{0,1:T(8,128)(4,1)} %compare_and_fusion) | copy-start | bytes 196612
  207.0 5.3 copy-start.6
  212.2 2.4 slice-start
  212.3 2.4 copy-start.5
  212.3 3.0 slice-start.1
  215.3 18.0 %copy-start.11 = (f32[1536]{0:T(1024)S(1)}, f32[1536]{0:T(1024)}, u32[]{:S(2)}) copy-start(f32[1536]{0:T(1024)} %param.17) | copy-start | bytes 18436
  233.2 641.1 %copy-start.3 = (bf16[128,1536]{1,0:T(8,128)(2,1)}, bf16[128,1536]{1,0:T(8,128)(2,1)S(1)}, u32[]{:S(2)}) copy-start(bf16[128,1536]{1,0:T(8,128)(2,1)S(1)} %get-tuple-element.26) | copy-start | bytes 1179652
  428.6 4.3 copy-start.13
  591.1 6.4 copy-start.12
  591.1 6.6 copy-start.10
  591.1 181.0 %all-to-all-start.1 = ((bf16[64,2,30720]{2,1,0:T(2,128)(2,1)}), bf16[64,2,30720]{2,1,0:T(2,128)(2,1)}, u32[]{:S(2)}, u32[]{:S(2)}) async-start(bf16[64,2,30720]{2,1,0:T(2,128)(2,1)} %reshape.394), calls=%async_computation.1 | async-start | bytes 15728640 | tf_op jit(solution)/shard_map/all_to_all | solution.py:167
  852.6 22.6 %copy-start.1 = (bf16[1,1536,512]{2,1,0:T(8,128)(2,1)S(1)}, bf16[1,1536,512]{2,1,0:T(8,128)(2,1)}, u32[]{:S(2)}) copy-start(bf16[1,1536,512]{2,1,0:T(8,128)(2,1)} %param.20) | copy-start | bytes 4718596
Sparse Core Ops, SparseCore 0:
  10.8 80.9 all-gather.8
  93.6 78.4 all-gather.4
  173.9 56.0 all-gather.6
where the time goes:
time: 890 us; the launch traced here: 882 us
  waiting for transfers between devices  323 us (36%)
  local copies, waits for them, and re-layouts  222 us (25%)
  blocking collectives  186 us (21%)
  other arithmetic  96.3 us (11%)
  matrix products  26.4 us (3%)
  between operations  14.5 us (2%)
  starting transfers between devices  14.1 us (2%)
    all_to_all x1, blocking collectives, shards(): lax.all_to_all(outgoing.reshape(total_units, CAP, model), 'tensor', split...  186 us
    all_to_all x1, waiting for transfers between devices, shards(): lax.all_to_all(produced, 'tensor', split_axis=1, concat_axis=0, tiled=True)  174 us
    convert_element_type x1, local copies, waits for them, and re-layouts, shards(): produced = jnp.einsum('erf,efd->erd', activated, expert_out, preferred_el...  86.3 us
    all_gather x1, waiting for transfers between devices, shards(): lax.all_gather(qkv_weight, 'dp', axis=1, tiled=True)  69.1 us
    unnamed x37, local copies, waits for them, and re-layouts  69.1 us
    all_gather x1, waiting for transfers between devices, shards(): piece = lax.all_gather(prefix_cache[0], 'tensor', axis=0, tiled=True)  57.4 us
    unnamed x2, other arithmetic  51.5 us
    reduce_sum x1, other arithmetic, shards(): jnp.einsum('tk,tksd->td', gate_weights[0], picked.astype(jnp.float32))  18.9 us
  transfers between devices with their start and end apart: 6, of which 6 were waited for; matrix products, arithmetic and copies ran while one was open for 7% of the time, Pallas kernels for 0%

commit v1 on v0

--- a/solution.py
+++ b/solution.py
@@ -109,7 +109,10 @@
         jnp.zeros((rows, KV_HEADS, ratio), jnp.float32),
         jnp.zeros((rows, KV_HEADS, ratio, HEAD_DIM), jnp.float32),
     )
-    piece = lax.all_gather(prefix_cache[0], "tensor", axis=0, tiled=True)
+    piece = jnp.concatenate(
+        lax.all_to_all(jnp.stack([prefix_cache[0]] * lax.axis_size("tensor")), "tensor", 0, 0),
+        axis=0,
+    )
     count = piece.shape[0]
     cached_keys = piece[:, 0].reshape(count, KV_HEADS, HEAD_DIM)
     cached_values = piece[:, 1].reshape(count, KV_HEADS, HEAD_DIM)

time: 890 us -> 813 us (0.913)
  waiting for transfers between devices: 323 us -> 240 us
  starting transfers between devices: 14.1 us -> 27.1 us
    all_gather x1 -> x0, waiting for transfers between devices: 57.4 us -> none  [shards(): piece = lax.all_gather(prefix_cache[0], 'tensor', axis=0, tiled=True)]
    all_gather x1, waiting for transfers between devices: 69.1 us -> 40.1 us  [shards(): lax.all_gather(qkv_weight, 'dp', axis=1, tiled=True)]
    all_to_all x0 -> x1, starting transfers between devices: none -> 13.2 us  [shards(): lax.all_to_all(jnp.stack([prefix_cache[0]] * lax.axis_size('tensor')), 't...]
    unnamed x37 -> x39, local copies, waits for them, and re-layouts: 69.1 us -> 69 us
where the time goes in v1:
time: 813 us; the launch traced here: 805 us
  waiting for transfers between devices  240 us (30%)
  local copies, waits for them, and re-layouts  216 us (27%)
  blocking collectives  186 us (23%)
  other arithmetic  94.6 us (12%)
  starting transfers between devices  27.1 us (3%)
  matrix products  26.3 us (3%)
  between operations  14.8 us (2%)
    all_to_all x1, blocking collectives, shards(): lax.all_to_all(outgoing.reshape(total_units, CAP, model), 'tensor', split...  186 us
    all_to_all x1, waiting for transfers between devices, shards(): lax.all_to_all(produced, 'tensor', split_axis=1, concat_axis=0, tiled=True)  174 us
    convert_element_type x1, local copies, waits for them, and re-layouts, shards(): produced = jnp.einsum('erf,efd->erd', activated, expert_out, preferred_el...  86.3 us
    unnamed x39, local copies, waits for them, and re-layouts  69 us
    unnamed x2, other arithmetic  51.5 us
    all_gather x1, waiting for transfers between devices, shards(): lax.all_gather(qkv_weight, 'dp', axis=1, tiled=True)  40.1 us
    reduce_sum x1, other arithmetic, shards(): jnp.einsum('tk,tksd->td', gate_weights[0], picked.astype(jnp.float32))  18.9 us
    gather x1, local copies, waits for them, and re-layouts, shards(): returned.reshape(total_units * CAP, model)[target]  17.6 us
  transfers between devices with their start and end apart: 6, of which 6 were waited for; matrix products, arithmetic and copies ran while one was open for 7% of the time, Pallas kernels for 0%

profile of v1, /device:TPU:1, one launch (start us, length us, event | category | flops | bytes accessed | tf_op | source)
XLA Modules:
  0.0 804.9 jit_solution(8139650020458573634)
XLA Ops:
  9.8 13.2 %all-to-all-start = ((bf16[64,8,2,512]{3,1,2,0:T(8,128)(2,1)}), bf16[64,8,2,512]{3,1,2,0:T(8,128)(2,1)}, u32[]{:S(2)}, u32[]{:S(2)}) async-start(bf16[64,8,2,512]{3,1,2,0:T(8,128)(2,1)} %stack.9), calls=%async_computation | async-start | bytes 2097152 | tf_op jit(solution)/shard_map/all_to_all | solution.py:113
  24.9 9.0 %reduce-window.19 = s32[32,8,128]{2,1,0:T(8,128)S(1)} reduce-window(s32[32,8,128]{2,1,0:T(8,128)S(1)} %fusion.61, s32[]{:T(128)} %constant.24.clone.1), window={size=1x1x128 pad=0_0x0_0x127_0}, to_apply=%region_11.12 | reduce-window | flops 4161536 | bytes 262148 | tf_op jit(solution)/shard_map/reduce-window.2
  36.7 8.1 %scatter_custom_fusion = s32[2560]{0:T(1024)S(1)} fusion(s32[2048]{0:T(1024)S(1)} %bitcast.189, s32[2048]{0:T(1024)S(1)} %reshape.384, s32[]{:T(128)} %constant.23.clone.1), kind=kCustom, calls=%fused_computation.94 | custom fusion | bytes 10244 | tf_op jit(solution)/shard_map/scatter | solution.py:159
  46.8 4.6 all-to-all-done
  54.9 40.1 %all-gather.3.cloned.1.call-done = bf16[1536,2560]{1,0:T(8,128)(2,1)} async-done(((bf16[1536,640]{1,0:T(8,128)(2,1)}), bf16[1536,2560]{1,0:T(8,128)(2,1)}) %all-gather.3.cloned.1.call-update) | async-done | bytes 7864336 | tf_op jit(solution)/shard_map/all_gather | solution.py:88
  94.9 4.5 convolution_convert_fusion.1
  101.3 3.8 collective-permute-start
  105.6 3.2 collective-permute-done
  109.9 3.7 collective-permute-start.1
  114.5 4.8 bitcast_reduce_fusion
  119.3 3.8 collective-permute-done.1
  126.6 2.1 copy.83
  129.8 3.7 fusion.3
  135.1 1.7 fusion.19
  138.1 1.7 fusion.37
  139.8 12.9 %all-gather.5.cloned.1.call-done = bf16[1536,1536]{1,0:T(8,128)(2,1)} async-done(((bf16[384,1536]{1,0:T(8,128)(2,1)}), bf16[1536,1536]{1,0:T(8,128)(2,1)}) %all-gather.5.cloned.1.call-update) | async-done | bytes 4718608 | tf_op jit(solution)/shard_map/all_gather | solution.py:89
  152.7 3.2 fusion.40
  156.2 9.5 %gather_fusion = bf16[2560,1536]{1,0:T(8,128)(2,1)} fusion(bf16[129,1536]{1,0:T(8,128)(2,1)S(1)} %concatenate.37, s32[3072]{0:T(1024)S(1)} %copy-done.9), kind=kCustom, calls=%fused_computation | custom fusion | bytes 15738880 | tf_op jit(solution)/shard_map/gather | solution.py:161
  165.7 185.6 %all_to_all.23 = bf16[64,40,1536]{2,1,0:T(8,128)(2,1)S(1)} all-to-all(bf16[64,40,1536]{2,1,0:T(8,128)(2,1)} %bitcast.169), channel_id=1, replica_groups=mesh['dp'=4,'tensor'=64] {'tensor'}, dimensions={0} | all-to-all | bytes 15728640 | tf_op jit(solution)/shard_map/all_to_all | solution.py:162
  351.2 4.2 convolution_bitcast_fusion
  355.5 2.3 fusion
  357.8 86.3 %copy.108 = bf16[1,2560,1536]{2,0,1:T(2,128)(2,1)} copy(bf16[1,2560,1536]{2,1,0:T(8,128)(2,1)S(1)} %fusion) | data formatting | bytes 15728640 | tf_op jit(solution)/shard_map/convert_element_type | solution.py:169
  444.7 51.5 %reduce.2 = bf16[2560,1536]{1,0:T(8,128)(2,1)} reduce(bf16[2560,1,1536]{2,1,0:T(2,128)(2,1)} %bitcast.167, bf16[]{:T(256)} %broadcast.285), dimensions={1}, to_apply=%bitcast.165.reduce_sub_computation | reduce | bytes 15728642
  496.2 17.6 %reshape.398 = bf16[64,2,30720]{2,1,0:T(2,128)(2,1)} reshape(bf16[2560,1536]{1,0:T(8,128)(2,1)} %reduce.2) | data formatting | bytes 15728640
  513.8 6.4 all-to-all-start.2
  520.4 174.4 %all-to-all-done.2 = bf16[64,2,30720]{2,1,0:T(2,128)(2,1)} async-done(((bf16[64,2,30720]{2,1,0:T(2,128)(2,1)}), bf16[64,2,30720]{2,1,0:T(2,128)(2,1)}, u32[]{:S(2)}, u32[]{:S(2)}) %all-to-all-start.2) | async-done | bytes 7864352 | tf_op jit(solution)/shard_map/all_to_all | solution.py:170
  694.8 38.0 %reshape.399 = bf16[2560,1,1536]{2,1,0:T(2,128)(2,1)} reshape(bf16[64,2,30720]{2,1,0:T(2,128)(2,1)} %all-to-all-done.2) | data formatting | bytes 15728640
  732.7 10.8 %copy.106 = bf16[1,2560,1536]{2,1,0:T(8,128)(2,1)} copy(bf16[1,2560,1536]{2,0,1:T(2,128)(2,1)} %bitcast.168) | data formatting | bytes 15728640
  743.6 17.6 %gather_fusion.1 = bf16[2048,1536]{1,0:T(8,128)(2,1)} fusion(bf16[2560,1536]{1,0:T(8,128)(2,1)} %bitcast.166, s32[2048]{0:T(1024)S(1)} %broadcast_clamp_fusion), kind=kCustom, calls=%fused_computation.1 | custom fusion | bytes 12591104 | tf_op jit(solution)/shard_map/gather | solution.py:171
  761.1 14.1 %reshape.363 = f32[128,8,2,1536]{3,2,1,0:T(2,128)} reshape(bf16[2048,1536]{1,0:T(8,128)(2,1)} %gather_fusion.1) | data formatting | bytes 18874368 | tf_op jit(solution)/shard_map/convert_element_type | solution.py:172
  775.3 18.9 %reduce_sum.89 = bf16[128,8,1536]{2,1,0:T(8,128)(2,1)} reduce(f32[128,8,2,1536]{3,2,1,0:T(2,128)} %reshape.363, f32[]{:T(128)} %constant.19.clone.1), dimensions={2}, to_apply=%region_15.16 | reduce | flops 1572864 | bytes 15728644 | tf_op jit(solution)/shard_map/tk,tksd->td/reduce_sum | solution.py:172
  794.1 2.8 fusion.72
  (111 shorter events, 26.1 us)
Async XLA Ops:
  7.2 344.1 %copy-start = (bf16[1,1536,512]{2,1,0:T(8,128)(2,1)S(1)}, bf16[1,1536,512]{2,1,0:T(8,128)(2,1)}, u32[]{:S(2)}) copy-start(bf16[1,1536,512]{2,1,0:T(8,128)(2,1)} %param.20) | copy-start | bytes 4718596
  7.2 16.5 %copy-start.11 = (s32[1,128,8]{1,2,0:T(8,128)S(1)}, s32[1,128,8]{1,2,0:T(8,128)}, u32[]{:S(2)}) copy-start(s32[1,128,8]{1,2,0:T(8,128)} %param.18) | copy-start | bytes 12292
  7.2 16.8 %copy-start.13 = (s32[1,256]{1,0:T(1,128)S(1)}, s32[1,256]{1,0:T(1,128)}, u32[]{:S(2)}) copy-start(s32[1,256]{1,0:T(1,128)} %param.16) | copy-start | bytes 3076
  7.2 37.8 %copy-start.2 = (bf16[1,128,1536]{2,1,0:T(8,128)(2,1)S(1)}, bf16[1,128,1536]{2,1,0:T(8,128)(2,1)}, u32[]{:S(2)}) copy-start(bf16[1,128,1536]{2,1,0:T(8,128)(2,1)} %param.11) | copy-start | bytes 1179652
  7.2 87.7 %all-gather.3.cloned.1.call-start = ((), (), s32[]{:S(2)}) async-start(), calls=%async_computation.3 | async-start | bytes 9830400 | tf_op jit(solution)/shard_map/all_gather | solution.py:88
  9.8 41.6 %all-to-all-start = ((bf16[64,8,2,512]{3,1,2,0:T(8,128)(2,1)}), bf16[64,8,2,512]{3,1,2,0:T(8,128)(2,1)}, u32[]{:S(2)}, u32[]{:S(2)}) async-start(bf16[64,8,2,512]{3,1,2,0:T(8,128)(2,1)} %stack.9), calls=%async_computation | async-start | bytes 2097152 | tf_op jit(solution)/shard_map/all_to_all | solution.py:113
  22.9 72.0 %copy-start.8 = (f32[1536]{0:T(1024)S(1)}, f32[1536]{0:T(1024)}, u32[]{:S(2)}) copy-start(f32[1536]{0:T(1024)} %param.12) | copy-start | bytes 18436
  23.0 129.7 %all-gather.5.cloned.1.call-start = ((), (), s32[]{:S(2)}) async-start(), calls=%async_computation.4 | async-start | bytes 5898240 | tf_op jit(solution)/shard_map/all_gather | solution.py:89
  35.5 0.6 copy-start.7
  101.3 7.4 collective-permute-start
  109.9 13.1 %collective-permute-start.1 = (bf16[2,128,2,512]{3,1,2,0:T(8,128)(2,1)S(1)}, bf16[2,128,2,512]{3,1,2,0:T(8,128)(2,1)S(1)}, u32[]{:S(2)}, u32[]{:S(2)}) collective-permute-start(bf16[2,128,2,512]{3,1,2,0:T(8,128)(2,1)S(1)} %pad_maximum_fusion.1), channel_id=1, source_target_pairs={{0,2},{1,3},{2,4},{3,5},{4,6},{5,7},{6,8},{7,9},{8,10},{9,11},{10,... | collective-permute-start | bytes 1572872 | tf_op jit(solution)/shard_map/ppermute | solution.py:20
  114.5 14.2 %copy-start.4 = (pred[128,512]{0,1:T(8,128)(4,1)S(1)}, pred[128,512]{0,1:T(8,128)(4,1)}, u32[]{:S(2)}) copy-start(pred[128,512]{0,1:T(8,128)(4,1)} %compare_and_fusion) | copy-start | bytes 196612
  129.8 5.3 copy-start.6
  135.0 2.4 slice-start
  135.0 2.4 copy-start.5
  135.1 3.0 slice-start.1
  138.1 17.9 %copy-start.10 = (f32[1536]{0:T(1024)S(1)}, f32[1536]{0:T(1024)}, u32[]{:S(2)}) copy-start(f32[1536]{0:T(1024)} %param.17) | copy-start | bytes 18436
  138.1 18.1 %copy-start.9 = (s32[3072]{0:T(1024)S(1)}, s32[3072]{0:T(1024)}, u32[]{:S(2)}) copy-start(s32[3072]{0:T(1024)} %pad_clamp_fusion) | copy-start | bytes 36868
  155.9 641.1 %copy-start.3 = (bf16[128,1536]{1,0:T(8,128)(2,1)}, bf16[128,1536]{1,0:T(8,128)(2,1)S(1)}, u32[]{:S(2)}) copy-start(bf16[128,1536]{1,0:T(8,128)(2,1)S(1)} %get-tuple-element.26) | copy-start | bytes 1179652
  351.2 4.3 copy-start.14
  513.8 6.4 copy-start.12
  513.8 180.9 %all-to-all-start.2 = ((bf16[64,2,30720]{2,1,0:T(2,128)(2,1)}), bf16[64,2,30720]{2,1,0:T(2,128)(2,1)}, u32[]{:S(2)}, u32[]{:S(2)}) async-start(bf16[64,2,30720]{2,1,0:T(2,128)(2,1)} %reshape.398), calls=%async_computation.2 | async-start | bytes 15728640 | tf_op jit(solution)/shard_map/all_to_all | solution.py:170
  775.3 22.6 %copy-start.1 = (bf16[1,1536,512]{2,1,0:T(8,128)(2,1)S(1)}, bf16[1,1536,512]{2,1,0:T(8,128)(2,1)}, u32[]{:S(2)}) copy-start(bf16[1,1536,512]{2,1,0:T(8,128)(2,1)} %param.20) | copy-start | bytes 4718596
Sparse Core Ops, SparseCore 0:
  9.9 85.0 all-gather.2
  96.7 55.8 all-gather.4
